TPU v7x, 256 devices: a whole 4x4x8 slice. The times are simulated.
256 devices in a mesh: pair: 64 (over y, z, core), aux: 4 (over x).
Axes of the slice: x: 4, y: 4, z: 8, core: 2. Of those that a mesh axis runs over, the one named last changes fastest.
Arguments:
- factors: bfloat16 [64, 8192, 8, 128], P('pair', 'aux'), may hold values from -0.0625 to 0.0625
- amplitudes: bfloat16 [3072, 128, 128], P('pair'), may hold values from -6 to 6
- block_list: int32 [3072, 3], P('pair'), may hold values from 0 to 63, as said below
- owner_map: int32 [64], replicated, may hold values from 0 to 63, as said below
Outputs:
- residual_blocks: bfloat16 [3072, 128, 128], P('pair')
Inputs may be any that keep to these rules, and one draw needn't show every extreme that they name: `block_list`: each row (k, A, C) names an occupied orbital below 64 and two virtual blocks below 8; no row repeats. Among the 48 rows of one device at most 2 have orbitals with the same owner_map entry, and exactly 2 for some entry on every device. `owner_map`: A permutation: entry k is the row of factors that holds orbital k.
All inputs are finite; a program needn't handle non-finite values.
Results may differ from a plain program's by a relative error of at most 0.0046.
Values may be sent and summed in bfloat16 or wider, within the bound.
A program may use at most 64 MiB of HBM per device.

v0:
```python
import jax
import jax.numpy as jnp
from jax import lax
from jax.sharding import PartitionSpec as P

CAP = 2


def on_device(factors, amplitudes, block_list, owner_map):
    pair_count = lax.axis_size("pair")
    slot_total = pair_count * CAP
    block_count = amplitudes.shape[0]
    block_width = amplitudes.shape[1]
    virt_blocks = factors.shape[2]
    share_rows = factors.shape[1]
    orbital_total = owner_map.shape[0]
    orbitals = block_list[:, 0]
    block_a = block_list[:, 1]
    block_c = block_list[:, 2]
    matches = orbitals[:, None] == lax.iota(jnp.int32, orbital_total)[None, :]
    owners = jnp.sum(jnp.where(matches, owner_map[None, :], 0), axis=1)
    owner_hits = (owners[:, None] == lax.iota(jnp.int32, pair_count)[None, :]).astype(jnp.int32)
    earlier = jnp.cumsum(owner_hits, axis=0) - owner_hits
    slot_rank = jnp.sum(earlier * owner_hits, axis=1)
    slots = owners * CAP + slot_rank
    placing = slots[:, None] == lax.iota(jnp.int32, slot_total)[None, :]
    place_matrix = placing.astype(jnp.bfloat16)
    flat_blocks = amplitudes.reshape(block_count, block_width * block_width)
    send_blocks = jnp.einsum(
        "js,jm->sm", place_matrix, flat_blocks, preferred_element_type=jnp.float32
    )
    send_blocks = send_blocks.astype(jnp.bfloat16).reshape(
        pair_count, CAP, block_width, block_width
    )
    send_a = jnp.sum(jnp.where(placing, block_a[:, None] + 1, 0), axis=0)
    send_c = jnp.sum(jnp.where(placing, block_c[:, None] + 1, 0), axis=0)
    send_index = (
        jnp.stack([send_a, send_c], axis=-1).astype(jnp.bfloat16).reshape(pair_count, CAP, 2)
    )
    recv_blocks, recv_index = (
        lax.all_to_all(send_blocks, "pair", split_axis=0, concat_axis=0, tiled=True),
        lax.all_to_all(send_index, "pair", split_axis=0, concat_axis=0, tiled=True),
    )
    recv_index = recv_index.reshape(slot_total, 2).astype(jnp.int32) - 1
    slot_a = recv_index[:, 0]
    slot_c = recv_index[:, 1]
    onehot_a = (slot_a[:, None] == lax.iota(jnp.int32, virt_blocks)[None, :]).astype(jnp.bfloat16)
    onehot_c = (slot_c[:, None] == lax.iota(jnp.int32, virt_blocks)[None, :]).astype(jnp.bfloat16)
    combined = (onehot_c[:, :, None] * onehot_a[:, None, :]).reshape(
        slot_total, virt_blocks * virt_blocks
    )
    recv_flat = recv_blocks.reshape(slot_total, block_width * block_width)
    weights = jnp.einsum("sm,sn->mn", combined, recv_flat, preferred_element_type=jnp.float32)
    weights = weights.reshape(virt_blocks, virt_blocks, block_width, block_width)
    weights = jnp.transpose(weights, (0, 3, 1, 2)).reshape(
        virt_blocks * block_width, virt_blocks * block_width
    )
    weights = weights.astype(jnp.bfloat16)
    factor_flat = factors.reshape(share_rows, virt_blocks * block_width)
    factor_rows = factor_flat
    inter_share = lax.psum_scatter(
        jnp.dot(factor_rows, weights, preferred_element_type=jnp.float32),
        "pair",
        scatter_dimension=0,
        tiled=True,
    )
    inter_share = inter_share.astype(jnp.bfloat16)
    shard_rows = lax.all_gather(inter_share, "pair", axis=0, tiled=True)
    height = shard_rows.shape[0]
    factor_rows = factor_flat
    left = shard_rows.reshape(height, virt_blocks, block_width)
    right = factor_rows.reshape(height, virt_blocks, block_width)
    projected = jnp.einsum("qAa,qCc->ACac", left, right, preferred_element_type=jnp.float32)
    safe_a = jnp.maximum(slot_a, 0)
    safe_c = jnp.maximum(slot_c, 0)
    summed = lax.psum(projected, "aux")
    picked = summed[safe_a, safe_c].astype(jnp.bfloat16)
    picked = picked.reshape(pair_count, CAP, block_width, block_width)
    returned = lax.all_to_all(picked, "pair", split_axis=0, concat_axis=0, tiled=True)
    returned = returned.reshape(slot_total, block_width * block_width)
    result = jnp.einsum("js,sm->jm", place_matrix, returned, preferred_element_type=jnp.float32)
    return result.astype(jnp.bfloat16).reshape(block_count, block_width, block_width)


def solution(mesh):
    placed = (P("pair", "aux", None, None), P("pair", None, None), P("pair", None), P())
    return jax.shard_map(
        on_device, mesh=mesh, in_specs=placed, out_specs=P("pair", None, None), check_vma=False
    )
```

profile of v0, /device:TPU:1, one launch (start us, length us, event | category | flops | bytes accessed | tf_op | source)
XLA Modules:
  0.0 617.8 jit_solution(2545537378293932037)
XLA Ops:
  6.5 0.8 add_bitcast_fusion
  7.3 0.8 select_reduce_fusion.3
  8.3 0.2 select_reduce_fusion.2
  8.7 0.1 stack.10
  8.8 0.2 stack.9
  9.0 0.7 copy.26
  9.6 13.2 %all-to-all-start = ((bf16[64,2,2]{1,2,0:T(2,128)(2,1)}), bf16[64,2,2]{1,2,0:T(2,128)(2,1)S(1)}, u32[]{:S(2)}, u32[]{:S(2)}) async-start(bf16[64,2,2]{1,2,0:T(2,128)(2,1)} %copy.26), calls=%async_computation | async-start | bytes 65536 | tf_op jit(solution)/shard_map/all_to_all | solution.py:42
  22.8 2.8 fusion.10
  25.6 3.2 copy.39
  28.8 3.2 all-to-all-done
  32.0 7.3 %all-to-all-start.1 = ((bf16[64,2,128,128]{3,2,1,0:T(8,128)(2,1)}), bf16[64,2,128,128]{3,2,1,0:T(8,128)(2,1)}, u32[]{:S(2)}, u32[]{:S(2)}) async-start(bf16[64,2,128,128]{3,2,1,0:T(8,128)(2,1)} %bitcast.84), calls=%async_computation.1 | async-start | bytes 8388608 | tf_op jit(solution)/shard_map/all_to_all | solution.py:41
  39.3 0.2 reduce-scatter.4.cloned.1.call-start
  39.7 0.1 copy.28
  39.8 0.1 sub.11
  40.0 95.3 %all-to-all-done.1 = bf16[64,2,128,128]{3,2,1,0:T(8,128)(2,1)} async-done(((bf16[64,2,128,128]{3,2,1,0:T(8,128)(2,1)}), bf16[64,2,128,128]{3,2,1,0:T(8,128)(2,1)}, u32[]{:S(2)}, u32[]{:S(2)}) %all-to-all-start.1) | async-done | bytes 4194336 | tf_op jit(solution)/shard_map/all_to_all | solution.py:41
  135.2 7.7 %copy.70 = bf16[16,8,128,128]{3,1,2,0:T(8,128)(2,1)} copy(bf16[16,8,128,128]{3,2,1,0:T(8,128)(2,1)} %bitcast.39) | data formatting | bytes 8388608
  142.9 6.4 %copy.29 = bf16[128,16384]{0,1:T(8,128)(2,1)} copy(bf16[128,16384]{1,0:T(8,128)(2,1)} %bitcast.88) | data formatting | bytes 8388608 | tf_op jit(solution)/shard_map/reshape | solution.py:52
  149.3 3.8 convert_bitcast_fusion
  153.1 3.3 copy.30
  156.3 10.6 %convolution_bitcast_fusion = f32[2048,1024]{0,1:T(8,128)} fusion(bf16[256,8,8,128]{3,2,1,0:T(8,128)(2,1)} %bitcast.92, bf16[128,8,8,128]{3,2,1,0:T(8,128)(2,1)} %bitcast.90), kind=kOutput, calls=%fused_computation.3 | convolution fusion | flops 4294967296 | bytes 14680064 | tf_op jit(solution)/shard_map/dot_general | solution.py:62
  166.9 9.3 %copy.36 = f32[2048,1024]{1,0:T(8,128)} copy(f32[2048,1024]{0,1:T(8,128)} %convolution_bitcast_fusion) | data formatting | bytes 16777216
  176.2 0.3 all-gather.2.cloned.1.call-start
  176.5 143.6 %reduce-scatter.4.cloned.1.call-done = f32[32,1024]{1,0:T(8,128)} async-done(((f32[2048,1024]{1,0:T(8,128)}), f32[32,1024]{1,0:T(8,128)}) %reduce-scatter.4.cloned.1.call-update) | async-done | bytes 131088 | tf_op jit(solution)/shard_map/reduce_scatter | solution.py:61
  320.2 1.5 convert_element_type.57
  321.7 83.6 %all-gather.2.cloned.1.call-done = bf16[2048,1024]{1,0:T(8,128)(2,1)} async-done(((bf16[32,1024]{1,0:T(8,128)(2,1)}), bf16[2048,1024]{1,0:T(8,128)(2,1)}) %all-gather.2.cloned.1.call-update) | async-done | bytes 4194320 | tf_op jit(solution)/shard_map/all_gather | solution.py:68
  405.3 6.5 %copy.32 = bf16[2048,1024]{0,1:T(8,128)(2,1)} copy(bf16[2048,1024]{1,0:T(8,128)(2,1)} %all-gather.2.cloned.1.call-done) | data formatting | bytes 8388608 | tf_op jit(solution)/shard_map/all_gather | solution.py:68
  411.8 9.9 %fusion.7 = f32[8,8,128,128]{3,2,1,0:T(8,128)} fusion(bf16[2048,8,128,1]{0,2,3,1:T(8,128)(2,1)} %bitcast.89, bf16[2048,8,128]{2,1,0:T(8,128)(2,1)} %bitcast.93), kind=kOutput, calls=%fused_computation.12 | convolution fusion | flops 4294967296 | bytes 12582912 | tf_op jit(solution)/shard_map/qAa,qCc->ACac/dot_general | solution.py:73
  421.7 78.1 %all-reduce.1 = bf16[8,8,128,128]{3,2,1,0:T(8,128)(2,1)S(1)} all-reduce(f32[8,8,128,128]{3,2,1,0:T(8,128)} %fusion.7), channel_id=1, replica_groups=mesh['pair'=64,'aux'=4] {'aux'}, use_global_device_ids=true, to_apply=%region_6.7 | all-reduce | flops 1048576 | bytes 6291456 | tf_op jit(solution)/shard_map/psum | solution.py:76
  499.8 3.1 gather_fusion
  502.8 103.9 %all_to_all.15 = bf16[64,2,128,128]{3,2,1,0:T(8,128)(2,1)S(1)} all-to-all(bf16[64,2,128,128]{3,2,1,0:T(8,128)(2,1)} %bitcast.86), channel_id=1, replica_groups=mesh['pair'=64,'aux'=4] {'pair'}, dimensions={0} | all-to-all | bytes 8388608 | tf_op jit(solution)/shard_map/all_to_all | solution.py:79
  606.7 2.7 fusion.15
  609.4 1.6 copy.44
  (13 shorter events, 0.4 us)
Async XLA Ops:
  9.6 22.4 %all-to-all-start = ((bf16[64,2,2]{1,2,0:T(2,128)(2,1)}), bf16[64,2,2]{1,2,0:T(2,128)(2,1)S(1)}, u32[]{:S(2)}, u32[]{:S(2)}) async-start(bf16[64,2,2]{1,2,0:T(2,128)(2,1)} %copy.26), calls=%async_computation | async-start | bytes 65536 | tf_op jit(solution)/shard_map/all_to_all | solution.py:42
  32.0 103.2 %all-to-all-start.1 = ((bf16[64,2,128,128]{3,2,1,0:T(8,128)(2,1)}), bf16[64,2,128,128]{3,2,1,0:T(8,128)(2,1)}, u32[]{:S(2)}, u32[]{:S(2)}) async-start(bf16[64,2,128,128]{3,2,1,0:T(8,128)(2,1)} %bitcast.84), calls=%async_computation.1 | async-start | bytes 8388608 | tf_op jit(solution)/shard_map/all_to_all | solution.py:41
  39.3 280.8 %reduce-scatter.4.cloned.1.call-start = ((), (), s32[]{:S(2)}) async-start(), calls=%async_computation.5 | async-start | bytes 8519680 | tf_op jit(solution)/shard_map/reduce_scatter | solution.py:61
  176.2 229.1 %all-gather.2.cloned.1.call-start = ((), (), s32[]{:S(2)}) async-start(), calls=%async_computation.4 | async-start | bytes 4259840 | tf_op jit(solution)/shard_map/all_gather | solution.py:68
Sparse Core Ops, SparseCore 0:
  176.4 143.7 reduce-scatter.3
  323.3 81.9 all-gather.1
where the time goes:
time: 619 us; the launch traced here: 618 us
  waiting for transfers between devices  326 us (53%)
  blocking collectives  182 us (29%)
  local copies, waits for them, and re-layouts  42.2 us (7%)
  matrix products  29.8 us (5%)
  starting transfers between devices  21 us (3%)
  between operations  13.5 us (2%)
    reduce_scatter x1, waiting for transfers between devices, on_device(): lax.psum_scatter(jnp.dot(factor_rows, weights, preferred_element_type=jnp...  144 us
    all_to_all x1, blocking collectives, on_device(): lax.all_to_all(picked, 'pair', split_axis=0, concat_axis=0, tiled=True)  104 us
    all_to_all x1, waiting for transfers between devices, on_device(): lax.all_to_all(send_blocks, 'pair', split_axis=0, concat_axis=0, tiled=True)  95.3 us
    all_gather x1, waiting for transfers between devices, on_device(): shard_rows = lax.all_gather(inter_share, 'pair', axis=0, tiled=True)  83.6 us
    psum x1, blocking collectives, on_device(): summed = lax.psum(projected, 'aux')  78.1 us
    unnamed x4, local copies, waits for them, and re-layouts  21.7 us
    all_to_all x1, starting transfers between devices, on_device(): lax.all_to_all(send_index, 'pair', split_axis=0, concat_axis=0, tiled=True)  13.2 us
  transfers between devices with their start and end apart: 4, of which 4 were waited for; matrix products, arithmetic and copies ran while one was open for 1% of the time, Pallas kernels for 0%

commit v1 on v0

--- a/solution.py
+++ b/solution.py
@@ -1,9 +1,25 @@
+import functools
 import jax
 import jax.numpy as jnp
 from jax import lax
 from jax.sharding import PartitionSpec as P
 
 CAP = 2
+
+
+def cards_define(sheet, axis_tag):
+    return jnp.concatenate(
+        lax.all_to_all(
+            jnp.stack([sheet for _ in range(lax.axis_size(axis_tag))], axis=0),
+            axis_tag,
+            split_axis=0,
+            concat_axis=0,
+        ),
+        0,
+    )
+
+
+run_the_heaps = functools.partial(cards_define, axis_tag="pair")
 
 
 def on_device(factors, amplitudes, block_list, owner_map):
@@ -65,7 +81,7 @@
         tiled=True,
     )
     inter_share = inter_share.astype(jnp.bfloat16)
-    shard_rows = lax.all_gather(inter_share, "pair", axis=0, tiled=True)
+    shard_rows = run_the_heaps(inter_share)
     height = shard_rows.shape[0]
     factor_rows = factor_flat
     left = shard_rows.reshape(height, virt_blocks, block_width)

time: 619 us -> 635 us (1.026)
  blocking collectives: 182 us -> 290 us
  waiting for transfers between devices: 326 us -> 242 us
    all_to_all x0 -> x1, blocking collectives: none -> 108 us  [cards_define(): lax.all_to_all(jnp.stack([sheet for _ in range(lax.axis_size(axis_tag))],...]
    all_gather x1 -> x0, waiting for transfers between devices: 83.6 us -> none  [on_device(): shard_rows = lax.all_gather(inter_share, 'pair', axis=0, tiled=True)]
    all_gather x1 -> x0, local copies, waits for them, and re-layouts: 6.49 us -> none  [on_device(): shard_rows = lax.all_gather(inter_share, 'pair', axis=0, tiled=True)]
    unnamed x4 -> x7, local copies, waits for them, and re-layouts: 21.7 us -> 23.9 us
  transfers between devices with their start and end apart: 4 -> 3, of which waited for: 4 -> 3; matrix products, arithmetic and copies ran while one was open for 1% -> 1% of each run, Pallas kernels for 0% -> 0%
where the time goes in v1:
time: 635 us; the launch traced here: 634 us
  blocking collectives  290 us (46%)
  waiting for transfers between devices  242 us (38%)
  local copies, waits for them, and re-layouts  38.4 us (6%)
  matrix products  25.9 us (4%)
  starting transfers between devices  20.7 us (3%)
  between operations  13.5 us (2%)
    reduce_scatter x1, waiting for transfers between devices, on_device(): lax.psum_scatter(jnp.dot(factor_rows, weights, preferred_element_type=jnp...  144 us
    all_to_all x1, blocking collectives, cards_define(): lax.all_to_all(jnp.stack([sheet for _ in range(lax.axis_size(axis_tag))],...  108 us
    all_to_all x1, blocking collectives, on_device(): lax.all_to_all(picked, 'pair', split_axis=0, concat_axis=0, tiled=True)  104 us
    all_to_all x1, waiting for transfers between devices, on_device(): lax.all_to_all(send_blocks, 'pair', split_axis=0, concat_axis=0, tiled=True)  95.3 us
    psum x1, blocking collectives, on_device(): summed = lax.psum(projected, 'aux')  77.7 us
    unnamed x7, local copies, waits for them, and re-layouts  23.9 us
    all_to_all x1, starting transfers between devices, on_device(): lax.all_to_all(send_index, 'pair', split_axis=0, concat_axis=0, tiled=True)  13.2 us
  transfers between devices with their start and end apart: 3, of which 3 were waited for; matrix products, arithmetic and copies ran while one was open for 1% of the time, Pallas kernels for 0%

profile of v1, /device:TPU:1, one launch (start us, length us, event | category | flops | bytes accessed | tf_op | source)
XLA Modules:
  0.0 633.7 jit_solution(1588690074056042719)
XLA Ops:
  6.5 0.8 add_bitcast_fusion
  7.3 0.8 select_reduce_fusion.3
  8.3 0.2 select_reduce_fusion.2
  8.7 0.1 stack.9
  8.8 0.2 stack.8
  9.0 0.7 copy.28
  9.6 13.2 %all-to-all-start = ((bf16[64,2,2]{1,2,0:T(2,128)(2,1)}), bf16[64,2,2]{1,2,0:T(2,128)(2,1)S(1)}, u32[]{:S(2)}, u32[]{:S(2)}) async-start(bf16[64,2,2]{1,2,0:T(2,128)(2,1)} %copy.28), calls=%async_computation | async-start | bytes 65536 | tf_op jit(solution)/shard_map/all_to_all | solution.py:58
  22.8 2.8 fusion.13
  25.6 3.2 copy.43
  28.8 3.2 all-to-all-done
  32.0 7.3 %all-to-all-start.1 = ((bf16[64,2,128,128]{3,2,1,0:T(8,128)(2,1)}), bf16[64,2,128,128]{3,2,1,0:T(8,128)(2,1)}, u32[]{:S(2)}, u32[]{:S(2)}) async-start(bf16[64,2,128,128]{3,2,1,0:T(8,128)(2,1)} %bitcast.83), calls=%async_computation.1 | async-start | bytes 8388608 | tf_op jit(solution)/shard_map/all_to_all | solution.py:57
  39.3 0.2 reduce-scatter.4.cloned.1.call-start
  39.8 0.1 sub.11
  40.0 95.3 %all-to-all-done.1 = bf16[64,2,128,128]{3,2,1,0:T(8,128)(2,1)} async-done(((bf16[64,2,128,128]{3,2,1,0:T(8,128)(2,1)}), bf16[64,2,128,128]{3,2,1,0:T(8,128)(2,1)}, u32[]{:S(2)}, u32[]{:S(2)}) %all-to-all-start.1) | async-done | bytes 4194336 | tf_op jit(solution)/shard_map/all_to_all | solution.py:57
  135.2 7.7 %copy.79 = bf16[16,8,128,128]{3,1,2,0:T(8,128)(2,1)} copy(bf16[16,8,128,128]{3,2,1,0:T(8,128)(2,1)} %bitcast.35) | data formatting | bytes 8388608
  142.9 6.4 %copy.31 = bf16[128,16384]{0,1:T(8,128)(2,1)} copy(bf16[128,16384]{1,0:T(8,128)(2,1)} %bitcast.87) | data formatting | bytes 8388608 | tf_op jit(solution)/shard_map/reshape | solution.py:68
  149.3 3.8 convert_bitcast_fusion
  153.1 3.3 copy.32
  156.3 10.6 %convolution_bitcast_fusion = f32[2048,1024]{0,1:T(8,128)} fusion(bf16[256,8,8,128]{3,2,1,0:T(8,128)(2,1)} %bitcast.92, bf16[128,8,8,128]{3,2,1,0:T(8,128)(2,1)} %bitcast.90), kind=kOutput, calls=%fused_computation.3 | convolution fusion | flops 4294967296 | bytes 14680064 | tf_op jit(solution)/shard_map/dot_general | solution.py:78
  166.9 9.3 %copy.40 = f32[2048,1024]{1,0:T(8,128)} copy(f32[2048,1024]{0,1:T(8,128)} %convolution_bitcast_fusion) | data formatting | bytes 16777216
  176.2 143.9 %reduce-scatter.4.cloned.1.call-done = f32[32,1024]{1,0:T(8,128)} async-done(((f32[2048,1024]{1,0:T(8,128)}), f32[32,1024]{1,0:T(8,128)}) %reduce-scatter.4.cloned.1.call-update) | async-done | bytes 131088 | tf_op jit(solution)/shard_map/reduce_scatter | solution.py:77
  320.2 0.9 convert_element_type.57
  321.1 0.5 stack.11
  321.6 107.9 %all_to_all.20 = bf16[64,32,1024]{2,1,0:T(8,128)(2,1)S(1)} all-to-all(bf16[64,32,1024]{2,1,0:T(8,128)(2,1)S(1)} %stack.11), channel_id=1, replica_groups=mesh['pair'=64,'aux'=4] {'pair'}, dimensions={0} | all-to-all | bytes 8388608 | tf_op jit(solution)/shard_map/all_to_all | solution.py:12
  429.5 1.1 copy.47
  430.7 1.0 copy-done
  431.7 6.1 fusion.8
  437.8 77.7 %all-reduce.1 = bf16[8,8,128,128]{3,2,1,0:T(8,128)(2,1)S(1)} all-reduce(f32[8,8,128,128]{3,2,1,0:T(8,128)} %fusion.8), channel_id=1, replica_groups=mesh['pair'=64,'aux'=4] {'aux'}, use_global_device_ids=true, to_apply=%region_6.7 | all-reduce | flops 1048576 | bytes 6291456 | tf_op jit(solution)/shard_map/psum | solution.py:92
  515.4 3.1 gather_fusion
  518.5 104.1 %all_to_all.21 = bf16[64,2,128,128]{3,2,1,0:T(8,128)(2,1)S(1)} all-to-all(bf16[64,2,128,128]{3,2,1,0:T(8,128)(2,1)} %bitcast.85), channel_id=1, replica_groups=mesh['pair'=64,'aux'=4] {'pair'}, dimensions={0} | all-to-all | bytes 8388608 | tf_op jit(solution)/shard_map/all_to_all | solution.py:95
  622.6 2.7 fusion.18
  625.3 1.6 copy.49
  (14 shorter events, 0.5 us)
Async XLA Ops:
  9.6 22.4 %all-to-all-start = ((bf16[64,2,2]{1,2,0:T(2,128)(2,1)}), bf16[64,2,2]{1,2,0:T(2,128)(2,1)S(1)}, u32[]{:S(2)}, u32[]{:S(2)}) async-start(bf16[64,2,2]{1,2,0:T(2,128)(2,1)} %copy.28), calls=%async_computation | async-start | bytes 65536 | tf_op jit(solution)/shard_map/all_to_all | solution.py:58
  32.0 103.2 %all-to-all-start.1 = ((bf16[64,2,128,128]{3,2,1,0:T(8,128)(2,1)}), bf16[64,2,128,128]{3,2,1,0:T(8,128)(2,1)}, u32[]{:S(2)}, u32[]{:S(2)}) async-start(bf16[64,2,128,128]{3,2,1,0:T(8,128)(2,1)} %bitcast.83), calls=%async_computation.1 | async-start | bytes 8388608 | tf_op jit(solution)/shard_map/all_to_all | solution.py:57
  39.3 280.8 %reduce-scatter.4.cloned.1.call-start = ((), (), s32[]{:S(2)}) async-start(), calls=%async_computation.5 | async-start | bytes 8519680 | tf_op jit(solution)/shard_map/reduce_scatter | solution.py:77
  429.5 2.2 copy-start
Sparse Core Ops, SparseCore 0:
  176.4 143.7 reduce-scatter.3
